TPU v7x, 128 devices: a whole 4x4x4 slice. The times are simulated.
128 devices in a mesh: ctx: 4 (over z_lo, core), tp: 16 (over y, x), dp: 2 (over z_hi).
Axes of the slice: x: 4, y: 4, z: 4 (z_hi: 2, z_lo: 2; z = z_hi * 2 + z_lo), core: 2. Of those that a mesh axis runs over, the one named last changes fastest.
Arguments:
- hidden_in: bfloat16 [8192, 8192], P(('dp', 'ctx', 'tp')), parts along dimension 0
- norm_gain: float32 [8192], replicated
- q_weight: bfloat16 [8192, 8192], P(None, 'tp')
- kv_weight: bfloat16 [8192, 2048], P(None, 'tp')
- out_weight: bfloat16 [8192, 8192], P('tp'), may hold values from -0.25 to 0.25
- doc_lengths: int32 [16], P('dp'), parts along dimension 0, may hold values from 1 to 2048, 4096 in all
Outputs:
- attn_out: bfloat16 [8192, 8192], P(('dp', 'ctx', 'tp')), parts along dimension 0
There are 2 independent parts, one for each index of `dp`. A program takes and returns all parts, laid end to end along the dimension named above; an argument that names none is the same for every part. Nothing has to cross between parts.
Inputs may be any that keep to these rules, and one draw needn't show every extreme that they name: `doc_lengths`: the lengths of a row sum to 4096; the longest document has exactly 2048 tokens.
All inputs are finite; a program needn't handle non-finite values.
Results may differ from a plain program's by a relative error of at most 0.015.
The roundings to bfloat16 on the way count: a program that leaves them out, or rounds other values in their place, can miss the bound.
Values may be sent and summed in bfloat16 or wider, within the bound.
No kernel may reach another device: no remote copies, remote signals or barrier semaphores. Data moves between devices by JAX's collectives and lax.ppermute only.
A program may use at most 128 MiB of HBM per device.

v0:
```python
import math
import jax
import jax.numpy as jnp
from jax import lax
from jax.sharding import PartitionSpec as P

QH = 64
KVH = 8
HD = 128


def from_everyone(shard, axis):
    length = lax.axis_size(axis)
    return lax.all_to_all(
        jnp.broadcast_to(shard[None], (length, *shard.shape)), axis, 0, 0, tiled=True
    )


def laid_out(blocks, dim):
    blocks = jnp.moveaxis(blocks, 0, dim)
    shape = blocks.shape
    return blocks.reshape(*shape[:dim], shape[dim] * shape[dim + 1], *shape[dim + 2 :])


def gathered_copies(shard, axis, dim):
    blocks = from_everyone(shard, axis)
    return laid_out(blocks, dim)


def doc_index(positions, ends):
    return jnp.sum((positions[:, None] >= ends[None, :]).astype(jnp.int32), axis=1)


def doc_start(positions, lengths, ends):
    return jnp.sum(jnp.where(positions[:, None] >= ends[None, :], lengths[None, :], 0), axis=1)


def rope_freqs(half):
    base = jnp.power(jnp.float32(500000.0), -(jnp.arange(half, dtype=jnp.float32) * 2.0) / HD)
    wavelen = 2.0 * math.pi / base
    smooth = (8192.0 / wavelen - 1.0) / 3.0
    middle = (1.0 - smooth) * base / 8.0 + smooth * base
    return jnp.where(wavelen < 2048.0, base, jnp.where(wavelen > 8192.0, base / 8.0, middle))


def rotate(values, within):
    rows = values.shape[0]
    blocks = values.reshape(rows, values.shape[1] // HD, HD)
    half = HD // 2
    freqs = rope_freqs(half)
    angles = within.astype(jnp.float32)[:, None] * freqs[None, :]
    cosine = jnp.cos(angles)[:, None, :]
    sine = jnp.sin(angles)[:, None, :]
    first = blocks[:, :, :half]
    second = blocks[:, :, half:]
    turned = jnp.concatenate(
        [first * cosine - second * sine, second * cosine + first * sine], axis=2
    )
    return turned.reshape(rows, values.shape[1])


def local(hidden_in, norm_gain, q_weight, kv_weight, out_weight, doc_lengths):
    tok_rows = hidden_in.shape[0]
    n_tp = lax.axis_size("tp")
    n_ctx = lax.axis_size("ctx")
    ctx_rows = tok_rows * n_tp
    block_rows = ctx_rows // n_ctx
    q_cols = q_weight.shape[1]
    heads_here = q_cols // HD
    group = QH // KVH
    kv_here = max(1, heads_here // group)
    sub_heads = heads_here // kv_here
    kv_cols = kv_weight.shape[1]
    tp_index = lax.axis_index("tp")
    ctx_index = lax.axis_index("ctx")
    scale = HD ** (-0.5)
    x = hidden_in.astype(jnp.float32)
    normed = (
        x * lax.rsqrt(jnp.mean(x * x, axis=1, keepdims=True) + 1e-05) * norm_gain[None, :]
    ).astype(jnp.bfloat16)
    ends = jnp.cumsum(doc_lengths)
    is_key = tp_index * kv_cols < KVH * HD
    piece = lax.all_gather(normed, "tp", axis=0, tiled=True)
    count = piece.shape[0]
    positions = ctx_index * ctx_rows + jnp.arange(count, dtype=jnp.int32)
    within = positions - doc_start(positions, doc_lengths, ends)
    q_raw = jnp.dot(piece, q_weight, preferred_element_type=jnp.float32)
    kv_raw = jnp.dot(piece, kv_weight, preferred_element_type=jnp.float32)
    q_done = rotate(q_raw, within).astype(jnp.bfloat16)
    kv_done = jnp.where(is_key, rotate(kv_raw, within), kv_raw).astype(jnp.bfloat16)
    projected = jnp.concatenate([q_done, kv_done], axis=1)
    queries = projected[:, :q_cols]
    kv_part = projected[:, q_cols:]
    kv_every = lax.all_gather(kv_part, "tp", axis=1, tiled=True)
    first_kv = tp_index * heads_here // group
    key_cols = lax.dynamic_slice_in_dim(kv_every, first_kv * HD, kv_here * HD, 1)
    value_cols = lax.dynamic_slice_in_dim(kv_every, KVH * HD + first_kv * HD, kv_here * HD, 1)
    kv_mine = jnp.concatenate([key_cols, value_cols], axis=1)
    block_starts = [ctx_index * ctx_rows + b * block_rows for b in range(n_ctx)]
    q_blocks = queries.reshape(n_ctx, block_rows, kv_here, sub_heads, HD).transpose(0, 2, 3, 1, 4)
    q_positions = [
        start_row + jnp.arange(block_rows, dtype=jnp.int32) for start_row in block_starts
    ]
    q_docs = [doc_index(pos, ends) for pos in q_positions]
    piece = gathered_copies(kv_mine, "ctx", 0)
    top_all = jnp.full((n_ctx, kv_here, sub_heads, block_rows), -1e30, jnp.float32)
    total_all = jnp.zeros((n_ctx, kv_here, sub_heads, block_rows), jnp.float32)
    acc_all = jnp.zeros((n_ctx, kv_here, sub_heads, block_rows, HD), jnp.float32)
    count = piece.shape[0]
    key_piece = piece[:, : kv_here * HD].reshape(count, kv_here, HD)
    value_piece = piece[:, kv_here * HD :].reshape(count, kv_here, HD)
    key_pos = jnp.arange(count, dtype=jnp.int32)
    key_doc = doc_index(key_pos, ends)
    new_top = []
    new_total = []
    new_acc = []
    for block in range(n_ctx):
        q_here = q_blocks[block]
        q_pos = q_positions[block]
        q_doc = q_docs[block]
        state = (top_all[block], total_all[block], acc_all[block])
        top_old, total_old, acc_old = state
        scores = (
            jnp.einsum("ghqd,kgd->ghqk", q_here, key_piece, preferred_element_type=jnp.float32)
            * scale
        )
        visible = (key_doc[None, :] == q_doc[:, None]) & (key_pos[None, :] <= q_pos[:, None])
        scores = jnp.where(visible[None, None], scores, jnp.float32(-1e30))
        top_new = jnp.maximum(top_old, jnp.max(scores, axis=3))
        expd = jnp.where(
            visible[None, None], jnp.exp(scores - top_new[..., None]), jnp.float32(0.0)
        )
        total_new = jnp.sum(expd, axis=3)
        acc_new = jnp.einsum(
            "ghqk,kgd->ghqd",
            expd.astype(jnp.bfloat16),
            value_piece,
            preferred_element_type=jnp.float32,
        )
        state = (top_new, total_new, acc_new)
        new_top.append(state[0])
        new_total.append(state[1])
        new_acc.append(state[2])
    total_all = jnp.stack(new_total)
    acc_all = jnp.stack(new_acc)
    heads_out = (acc_all / total_all[..., None]).astype(jnp.bfloat16)
    heads_out = heads_out.transpose(0, 3, 1, 2, 4).reshape(ctx_rows, q_cols)
    return lax.psum_scatter(
        jnp.dot(heads_out, out_weight, preferred_element_type=jnp.float32).astype(jnp.bfloat16),
        "tp",
        scatter_dimension=0,
        tiled=True,
    )


def solution(mesh):
    placed = (
        P(("dp", "ctx", "tp"), None),
        P(),
        P(None, "tp"),
        P(None, "tp"),
        P("tp", None),
        P("dp"),
    )
    return jax.shard_map(
        local, mesh=mesh, in_specs=placed, out_specs=P(("dp", "ctx", "tp"), None), check_vma=False
    )
```

profile of v0, /device:TPU:1, one launch (start us, length us, event | category | flops | bytes accessed | tf_op | source)
XLA Modules:
  0.0 425.1 jit_solution(6359207053137103046)
XLA Ops:
  6.5 1.7 fusion.28
  8.2 2.5 fusion.30
  10.8 0.8 reduce-window.8
  12.5 112.6 %all-gather.3.cloned.1.call-done = bf16[1024,8192]{1,0:T(8,128)(2,1)} async-done(((bf16[64,8192]{1,0:T(8,128)(2,1)}), bf16[1024,8192]{1,0:T(8,128)(2,1)}) %all-gather.3.cloned.1.call-update) | async-done | bytes 16777232 | tf_op jit(solution)/shard_map/all_gather | solution.py:83
  125.0 11.4 %fusion.73 = f32[1024,128]{0,1:T(8,128)S(1)} fusion(bf16[1024,8192]{1,0:T(8,128)(2,1)} %all-gather.3.cloned.1.call-done, bf16[8192,128]{1,0:T(8,128)(2,1)S(1)} %copy-done), kind=kOutput, calls=%fused_computation.116 | convolution fusion | flops 2147483648 | bytes 19398656 | tf_op jit(solution)/shard_map/dot_general | solution.py:88
  136.5 1.2 fusion.57
  138.7 3.1 multiply_cosine_fusion
  141.7 6.3 %fusion.24 = (pred[256,4096]{1,0:T(8,128)(4,1)}, pred[256,4096]{1,0:T(8,128)(4,1)}, pred[256,4096]{1,0:T(8,128)(4,1)}, pred[256,4096]{1,0:T(8,128)(4,1)S(1)}) fusion(s32[256]{0:T(256)S(1)} %iota_add_fusion.4, s32[4096]{0:T(1024)S(1)} %convert_reduce_fusion, s32[256]{0:T(256)S(1)} %get-tuple-element.5, s32[256]{0:T(256)S(1)} %iota_add_fusion.3, ...), kind=kLoop, calls=%fused_computation.33 | loop fusion | flops 12582912 | bytes 4218880 | tf_op jit(solution)/shard_map/and | solution.py:127
  148.1 41.5 %all-gather.5.cloned.1.call-done = bf16[1024,2048]{0,1:T(8,128)(2,1)} async-done(((bf16[1024,128]{0,1:T(8,128)(2,1)}), bf16[1024,2048]{0,1:T(8,128)(2,1)}) %all-gather.5.cloned.1.call-update) | async-done | bytes 4194320 | tf_op jit(solution)/shard_map/all_gather | solution.py:94
  189.6 1.1 constant_dynamic-slice_fusion.1
  190.9 1.4 broadcast_in_dim.65
  192.3 5.2 %all-to-all-start = ((bf16[4,1024,256]{2,1,0:T(8,128)(2,1)}), bf16[4,1024,256]{2,1,0:T(8,128)(2,1)}, u32[]{:S(2)}, u32[]{:S(2)}) async-start(bf16[4,1024,256]{2,1,0:T(8,128)(2,1)} %broadcast_in_dim.65), calls=%async_computation | async-start | bytes 4194304 | tf_op jit(solution)/shard_map/all_to_all | solution.py:14
  198.1 17.2 %fusion.72 = f32[1024,512]{0,1:T(8,128)S(1)} fusion(bf16[1024,8192]{1,0:T(8,128)(2,1)} %all-gather.3.cloned.1.call-done, bf16[8192,512]{1,0:T(8,128)(2,1)} %param.8), kind=kOutput, calls=%fused_computation.115 | convolution fusion | flops 8589934592 | bytes 27262976 | tf_op jit(solution)/shard_map/dot_general | solution.py:87
  215.3 1.6 fusion.71
  216.9 1.8 copy.19
  218.7 3.2 copy.18
  221.9 2.4 subtract_convert_fusion
  224.9 1.1 copy.26
  226.0 5.0 %fusion = (f32[4,256]{1,0:T(4,128)S(1)}, f32[4,256,4096]{2,1,0:T(8,128)S(1)}) fusion(pred[256,4096]{1,0:T(8,128)(4,1)} %get-tuple-element.17, bf16[4096,256]{1,0:T(8,128)(2,1)} %bitcast.8, bf16[4,1,4,256,128]{4,3,2,1,0:T(8,128)(2,1)} %bitcast.85), kind=kOutput, calls=%fused_computation.9 | convolution fusion | flops 1086323712 | bytes 19140608 | tf_op jit(solution)/shard_map/ghqd,kgd->ghqk/dot_general | solution.py:124
  231.0 5.2 %fusion.4 = f32[4,256]{1,0:T(4,128)S(1)} fusion(f32[4,256,4096]{2,1,0:T(8,128)S(1)} %get-tuple-element.30, f32[4,256]{1,0:T(4,128)S(1)} %broadcast_maximum_fusion.3, pred[256,4096]{1,0:T(8,128)(4,1)S(1)} %copy-done.4), kind=kLoop, calls=%fused_computation.13 | loop fusion | flops 20970496 | bytes 17833984 | tf_op jit(solution)/shard_map/reduce_sum | solution.py:133
  236.3 6.3 %fusion.32 = f32[1,1,4,256,128]{4,3,2,1,0:T(8,128)S(1)} fusion(f32[4,256,4096]{2,1,0:T(8,128)S(1)} %get-tuple-element.30, f32[4,256]{1,0:T(4,128)S(1)} %broadcast_maximum_fusion.3, pred[256,4096]{1,0:T(8,128)(4,1)S(1)} %copy-done.5, bf16[4096,256]{1,0:T(8,128)(2,1)} %bitcast.8), kind=kOutput, calls=%fused_computation.46 | convolution fusion | flops 1094713344 | bytes 19402752 | tf_op jit(solution)/shard_map/ghqk,kgd->ghqd/dot_general | solution.py:134
  242.6 4.7 %fusion.1 = (f32[4,256]{1,0:T(4,128)S(1)}, f32[4,256,4096]{2,1,0:T(8,128)S(1)}) fusion(pred[256,4096]{1,0:T(8,128)(4,1)S(1)} %copy-done.3, bf16[4096,256]{1,0:T(8,128)(2,1)} %bitcast.8, bf16[4,1,4,256,128]{4,3,2,1,0:T(8,128)(2,1)S(1)} %bitcast.86), kind=kOutput, calls=%fused_computation.10 | convolution fusion | flops 1086323712 | bytes 19140608 | tf_op jit(solution)/shard_map/ghqd,kgd->ghqk/dot_general | solution.py:124
  247.3 5.3 %fusion.6 = f32[4,256]{1,0:T(4,128)S(1)} fusion(f32[4,256,4096]{2,1,0:T(8,128)S(1)} %get-tuple-element.28, f32[4,256]{1,0:T(4,128)S(1)} %broadcast_maximum_fusion.2, pred[256,4096]{1,0:T(8,128)(4,1)S(1)} %copy-done.3), kind=kLoop, calls=%fused_computation.15 | loop fusion | flops 20970496 | bytes 17833984 | tf_op jit(solution)/shard_map/reduce_sum | solution.py:133
  252.6 6.2 %fusion.35 = f32[1,1,4,256,128]{4,3,2,1,0:T(8,128)S(1)} fusion(f32[4,256,4096]{2,1,0:T(8,128)S(1)} %get-tuple-element.28, f32[4,256]{1,0:T(4,128)S(1)} %broadcast_maximum_fusion.2, pred[256,4096]{1,0:T(8,128)(4,1)S(1)} %copy-done.3, bf16[4096,256]{1,0:T(8,128)(2,1)} %bitcast.8), kind=kOutput, calls=%fused_computation.47 | convolution fusion | flops 1094713344 | bytes 19402752 | tf_op jit(solution)/shard_map/ghqk,kgd->ghqd/dot_general | solution.py:134
  258.8 4.7 %fusion.2 = (f32[4,256]{1,0:T(4,128)S(1)}, f32[4,256,4096]{2,1,0:T(8,128)S(1)}) fusion(pred[256,4096]{1,0:T(8,128)(4,1)S(1)} %copy-done.2, bf16[4096,256]{1,0:T(8,128)(2,1)} %bitcast.8, bf16[4,1,4,256,128]{4,3,2,1,0:T(8,128)(2,1)S(1)} %bitcast.87), kind=kOutput, calls=%fused_computation.11 | convolution fusion | flops 1086323712 | bytes 19140608 | tf_op jit(solution)/shard_map/ghqd,kgd->ghqk/dot_general | solution.py:124
  263.6 5.3 %fusion.8 = f32[4,256]{1,0:T(4,128)S(1)} fusion(f32[4,256,4096]{2,1,0:T(8,128)S(1)} %get-tuple-element.26, f32[4,256]{1,0:T(4,128)S(1)} %broadcast_maximum_fusion.1, pred[256,4096]{1,0:T(8,128)(4,1)S(1)} %copy-done.2), kind=kLoop, calls=%fused_computation.17 | loop fusion | flops 20970496 | bytes 17833984 | tf_op jit(solution)/shard_map/reduce_sum | solution.py:133
  268.9 6.1 %fusion.38 = f32[1,1,4,256,128]{4,3,2,1,0:T(8,128)S(1)} fusion(f32[4,256,4096]{2,1,0:T(8,128)S(1)} %get-tuple-element.26, f32[4,256]{1,0:T(4,128)S(1)} %broadcast_maximum_fusion.1, pred[256,4096]{1,0:T(8,128)(4,1)S(1)} %copy-done.2, bf16[4096,256]{1,0:T(8,128)(2,1)} %bitcast.8), kind=kOutput, calls=%fused_computation.48 | convolution fusion | flops 1094713344 | bytes 19402752 | tf_op jit(solution)/shard_map/ghqk,kgd->ghqd/dot_general | solution.py:134
  275.0 4.7 %fusion.3 = (f32[4,256]{1,0:T(4,128)S(1)}, f32[4,256,4096]{2,1,0:T(8,128)S(1)}) fusion(pred[256,4096]{1,0:T(8,128)(4,1)S(1)} %get-tuple-element.20, bf16[4096,256]{1,0:T(8,128)(2,1)} %bitcast.8, bf16[4,1,4,256,128]{4,3,2,1,0:T(8,128)(2,1)S(1)} %bitcast.88), kind=kOutput, calls=%fused_computation.12 | convolution fusion | flops 1086323712 | bytes 19140608 | tf_op jit(solution)/shard_map/ghqd,kgd->ghqk/dot_general | solution.py:124
  279.7 6.1 %fusion.41 = f32[1,1,4,256,128]{4,3,2,1,0:T(8,128)S(1)} fusion(f32[4,256,4096]{2,1,0:T(8,128)S(1)} %get-tuple-element.24, f32[4,256]{1,0:T(4,128)S(1)} %broadcast_maximum_fusion, pred[256,4096]{1,0:T(8,128)(4,1)S(1)} %get-tuple-element.20, bf16[4096,256]{1,0:T(8,128)(2,1)} %bitcast.8), kind=kOutput, calls=%fused_computation.49 | convolution fusion | flops 1094713344 | bytes 19402752 | tf_op jit(solution)/shard_map/ghqk,kgd->ghqd/dot_general | solution.py:134
  285.9 5.3 %fusion.10 = f32[4,256]{1,0:T(4,128)S(1)} fusion(f32[4,256,4096]{2,1,0:T(8,128)S(1)} %get-tuple-element.24, f32[4,256]{1,0:T(4,128)S(1)} %broadcast_maximum_fusion, pred[256,4096]{1,0:T(8,128)(4,1)S(1)} %get-tuple-element.20), kind=kLoop, calls=%fused_computation.19 | loop fusion | flops 20970496 | bytes 17833984 | tf_op jit(solution)/shard_map/reduce_sum | solution.py:133
  292.8 15.3 %convolution_convert_fusion = bf16[1024,8192]{1,0:T(8,128)(2,1)} fusion(bf16[512,8192]{1,0:T(8,128)(2,1)} %param.10, bf16[128,8,4,128]{3,2,1,0:T(4,128)(2,1)S(1)} %bitcast.89), kind=kOutput, calls=%fused_computation.8 | convolution fusion | flops 8598323200 | bytes 26214400 | tf_op jit(solution)/shard_map/dot_general | solution.py:149
  308.1 110.0 %reduce-scatter.2.cloned.1.call-done = bf16[64,8192]{1,0:T(8,128)(2,1)} async-done(((bf16[1024,8192]{1,0:T(8,128)(2,1)}), bf16[64,8192]{1,0:T(8,128)(2,1)}) %reduce-scatter.2.cloned.1.call-update) | async-done | bytes 1048592 | tf_op jit(solution)/shard_map/reduce_scatter | solution.py:148
  (42 shorter events, 4.8 us)
Async XLA Ops:
  6.5 118.5 %copy-start = (bf16[8192,128]{1,0:T(8,128)(2,1)S(1)}, bf16[8192,128]{1,0:T(8,128)(2,1)}, u32[]{:S(2)}) copy-start(bf16[8192,128]{1,0:T(8,128)(2,1)} %param.9) | copy-start | bytes 6291460
  6.5 118.5 %all-gather.3.cloned.1.call-start = ((), (), s32[]{:S(2)}) async-start(), calls=%async_computation.2 | async-start | bytes 17825792 | tf_op jit(solution)/shard_map/all_gather | solution.py:83
  10.8 178.8 %all-gather.5.cloned.1.call-start = ((), (), s32[]{:S(2)}) async-start(), calls=%async_computation.3 | async-start | bytes 4456448 | tf_op jit(solution)/shard_map/all_gather | solution.py:94
  192.3 33.7 %all-to-all-start = ((bf16[4,1024,256]{2,1,0:T(8,128)(2,1)}), bf16[4,1024,256]{2,1,0:T(8,128)(2,1)}, u32[]{:S(2)}, u32[]{:S(2)}) async-start(bf16[4,1024,256]{2,1,0:T(8,128)(2,1)} %broadcast_in_dim.65), calls=%async_computation | async-start | bytes 4194304 | tf_op jit(solution)/shard_map/all_to_all | solution.py:14
  197.5 220.6 %reduce-scatter.2.cloned.1.call-start = ((), (), s32[]{:S(2)}) async-start(), calls=%async_computation.4 | async-start | bytes 17825792 | tf_op jit(solution)/shard_map/reduce_scatter | solution.py:148
  224.3 6.7 %copy-start.4 = (pred[256,4096]{1,0:T(8,128)(4,1)S(1)}, pred[256,4096]{1,0:T(8,128)(4,1)}, u32[]{:S(2)}) copy-start(pred[256,4096]{1,0:T(8,128)(4,1)} %get-tuple-element.17) | copy-start | bytes 3145732
  226.0 10.3 %copy-start.5 = (pred[256,4096]{1,0:T(8,128)(4,1)S(1)}, pred[256,4096]{1,0:T(8,128)(4,1)}, u32[]{:S(2)}) copy-start(pred[256,4096]{1,0:T(8,128)(4,1)} %get-tuple-element.17) | copy-start | bytes 3145732
  236.3 6.3 %copy-start.3 = (pred[256,4096]{1,0:T(8,128)(4,1)S(1)}, pred[256,4096]{1,0:T(8,128)(4,1)}, u32[]{:S(2)}) copy-start(pred[256,4096]{1,0:T(8,128)(4,1)} %get-tuple-element.18) | copy-start | bytes 3145732
  236.3 6.3 %copy-start.6 = (bf16[4,256,1,4,128]{4,1,3,2,0:T(8,128)(2,1)S(1)}, bf16[4,256,1,4,128]{4,1,3,2,0:T(8,128)(2,1)}, u32[]{:S(2)}) copy-start(bf16[4,256,1,4,128]{4,1,3,2,0:T(8,128)(2,1)} %copy.26) | copy-start | bytes 3145732
  252.6 6.2 %copy-start.2 = (pred[256,4096]{1,0:T(8,128)(4,1)S(1)}, pred[256,4096]{1,0:T(8,128)(4,1)}, u32[]{:S(2)}) copy-start(pred[256,4096]{1,0:T(8,128)(4,1)} %get-tuple-element.19) | copy-start | bytes 3145732
  292.8 125.3 %copy-start.1 = (bf16[8192,128]{1,0:T(8,128)(2,1)S(1)}, bf16[8192,128]{1,0:T(8,128)(2,1)}, u32[]{:S(2)}) copy-start(bf16[8192,128]{1,0:T(8,128)(2,1)} %param.9) | copy-start | bytes 6291460
Sparse Core Ops, SparseCore 0:
  10.9 114.0 all-gather.2
  138.5 50.9 all-gather.4
  308.2 109.8 reduce-scatter.1
where the time goes:
time: 432 us; the launch traced here: 425 us
  waiting for transfers between devices  264 us (61%)
  matrix products  87.8 us (20%)
  other arithmetic  42.2 us (10%)
  between operations  14 us (3%)
  local copies, waits for them, and re-layouts  11.2 us (3%)
  starting transfers between devices  5.8 us (1%)
    all_gather x1, waiting for transfers between devices, local(): piece = lax.all_gather(normed, 'tp', axis=0, tiled=True)  113 us
    reduce_scatter x1, waiting for transfers between devices, local(): lax.psum_scatter(jnp.dot(heads_out, out_weight, preferred_element_type=jn...  110 us
    all_gather x1, waiting for transfers between devices, local(): kv_every = lax.all_gather(kv_part, 'tp', axis=1, tiled=True)  41.5 us
    dot_general x4, matrix products, local(): jnp.einsum('ghqk,kgd->ghqd', expd.astype(jnp.bfloat16), value_piece, pref...  24.7 us
    reduce_sum x4, other arithmetic, local(): total_new = jnp.sum(expd, axis=3)  21.1 us
    dot_general x4, matrix products, local(): jnp.einsum('ghqd,kgd->ghqk', q_here, key_piece, preferred_element_type=jn...  19.2 us
    dot_general x1, matrix products, local(): q_raw = jnp.dot(piece, q_weight, preferred_element_type=jnp.float32)  17.2 us
    dot_general x1, matrix products, local(): jnp.dot(heads_out, out_weight, preferred_element_type=jnp.float32)  15.3 us
  transfers between devices with their start and end apart: 4, of which 3 were waited for; matrix products, arithmetic and copies ran while one was open for 9% of the time, Pallas kernels for 0%

commit v1 on v0

--- a/solution.py
+++ b/solution.py
@@ -80,7 +80,10 @@
     ).astype(jnp.bfloat16)
     ends = jnp.cumsum(doc_lengths)
     is_key = tp_index * kv_cols < KVH * HD
-    piece = lax.all_gather(normed, "tp", axis=0, tiled=True)
+    size = lax.axis_size("tp")
+    pieces = jnp.stack([normed for _ in range(size)])
+    pieces = lax.all_to_all(pieces, "tp", split_axis=0, concat_axis=0)
+    piece = jnp.concatenate(pieces, axis=0)
     count = piece.shape[0]
     positions = ctx_index * ctx_rows + jnp.arange(count, dtype=jnp.int32)
     within = positions - doc_start(positions, doc_lengths, ends)

time: 432 us -> 580 us (1.34)
  waiting for transfers between devices: 264 us -> 395 us
  local copies, waits for them, and re-layouts: 11.2 us -> 28.8 us
  starting transfers between devices: 5.8 us -> 13.3 us
    all_to_all x0 -> x1, waiting for transfers between devices: none -> 249 us  [local(): pieces = lax.all_to_all(pieces, 'tp', split_axis=0, concat_axis=0)]
    all_gather x1 -> x0, waiting for transfers between devices: 113 us -> none  [local(): piece = lax.all_gather(normed, 'tp', axis=0, tiled=True)]
    dot_general x0 -> x1, local copies, waits for them, and re-layouts: none -> 11.3 us  [local(): q_raw = jnp.dot(piece, q_weight, preferred_element_type=jnp.float32)]
    all_gather x1, waiting for transfers between devices: 41.5 us -> 32.2 us  [local(): kv_every = lax.all_gather(kv_part, 'tp', axis=1, tiled=True)]
    all_to_all x0 -> x1, starting transfers between devices: none -> 7.76 us  [local(): pieces = lax.all_to_all(pieces, 'tp', split_axis=0, concat_axis=0)]
    another operation x0 -> x1, local copies, waits for them, and re-layouts: none -> 5.93 us  [local(): pieces = jnp.stack([normed for _ in range(size)])]
  transfers between devices with their start and end apart: 4 -> 4, of which waited for: 3 -> 4; matrix products, arithmetic and copies ran while one was open for 9% -> 7% of each run, Pallas kernels for 0% -> 0%
where the time goes in v1:
time: 580 us; the launch traced here: 573 us
  waiting for transfers between devices  395 us (68%)
  matrix products  85.1 us (15%)
  other arithmetic  36.8 us (6%)
  local copies, waits for them, and re-layouts  28.8 us (5%)
  between operations  13.9 us (2%)
  starting transfers between devices  13.3 us (2%)
    all_to_all x1, waiting for transfers between devices, local(): pieces = lax.all_to_all(pieces, 'tp', split_axis=0, concat_axis=0)  249 us
    reduce_scatter x1, waiting for transfers between devices, local(): lax.psum_scatter(jnp.dot(heads_out, out_weight, preferred_element_type=jn...  111 us
    all_gather x1, waiting for transfers between devices, local(): kv_every = lax.all_gather(kv_part, 'tp', axis=1, tiled=True)  32.2 us
    dot_general x4, matrix products, local(): jnp.einsum('ghqk,kgd->ghqd', expd.astype(jnp.bfloat16), value_piece, pref...  24.6 us
    reduce_sum x4, other arithmetic, local(): total_new = jnp.sum(expd, axis=3)  20.8 us
    dot_general x4, matrix products, local(): jnp.einsum('ghqd,kgd->ghqk', q_here, key_piece, preferred_element_type=jn...  19.4 us
    dot_general x1, matrix products, local(): jnp.dot(heads_out, out_weight, preferred_element_type=jnp.float32)  15.3 us
    dot_general x1, matrix products, local(): q_raw = jnp.dot(piece, q_weight, preferred_element_type=jnp.float32)  14.4 us
  transfers between devices with their start and end apart: 4, of which 4 were waited for; matrix products, arithmetic and copies ran while one was open for 7% of the time, Pallas kernels for 0%

profile of v1, /device:TPU:1, one launch (start us, length us, event | category | flops | bytes accessed | tf_op | source)
XLA Modules:
  0.0 573.0 jit_solution(3448706338425159235)
XLA Ops:
  6.5 1.7 fusion.28
  8.2 1.5 fusion.30
  9.8 5.9 %stack.22 = bf16[16,64,8192]{2,1,0:T(8,128)(2,1)} broadcast(bf16[64,8192]{1,0:T(8,128)(2,1)S(1)} %fusion.30), dimensions={1,2} | broadcast | bytes 17825792 | tf_op jit(solution)/shard_map/stack | solution.py:84
  15.7 7.8 %all-to-all-start = ((bf16[16,64,8192]{2,1,0:T(8,128)(2,1)}), bf16[16,64,8192]{2,1,0:T(8,128)(2,1)}, u32[]{:S(2)}, u32[]{:S(2)}) async-start(bf16[16,64,8192]{2,1,0:T(8,128)(2,1)} %stack.22), calls=%async_computation | async-start | bytes 33554432 | tf_op jit(solution)/shard_map/all_to_all | solution.py:85
  23.9 248.7 %all-to-all-done = bf16[16,64,8192]{2,1,0:T(8,128)(2,1)} async-done(((bf16[16,64,8192]{2,1,0:T(8,128)(2,1)}), bf16[16,64,8192]{2,1,0:T(8,128)(2,1)}, u32[]{:S(2)}, u32[]{:S(2)}) %all-to-all-start) | async-done | bytes 16777248 | tf_op jit(solution)/shard_map/all_to_all | solution.py:85
  272.6 11.4 %fusion.72 = f32[1024,128]{0,1:T(8,128)S(1)} fusion(bf16[1024,8192]{1,0:T(8,128)(2,1)} %bitcast.2, bf16[8192,128]{1,0:T(8,128)(2,1)S(1)} %copy-done), kind=kOutput, calls=%fused_computation.114 | convolution fusion | flops 2147483648 | bytes 19398656 | tf_op jit(solution)/shard_map/dot_general | solution.py:91
  284.0 1.2 fusion.57
  286.0 11.3 %copy.18 = bf16[512,8192]{1,0:T(8,128)(2,1)} copy(bf16[512,8192]{0,1:T(8,128)(2,1)} %bitcast.85) | data formatting | bytes 16777216 | tf_op jit(solution)/shard_map/dot_general | solution.py:90
  297.5 1.7 multiply_cosine_fusion.1
  299.3 5.6 fusion.24
  304.8 32.2 %all-gather.2.cloned.1.call-done = bf16[1024,2048]{0,1:T(8,128)(2,1)} async-done(((bf16[1024,128]{0,1:T(8,128)(2,1)}), bf16[1024,2048]{0,1:T(8,128)(2,1)}) %all-gather.2.cloned.1.call-update) | async-done | bytes 4194320 | tf_op jit(solution)/shard_map/all_gather | solution.py:97
  339.0 2.1 copy.16
  341.1 2.5 broadcast_in_dim.65
  343.6 5.3 all-to-all-start.1
  349.1 14.4 %fusion.71 = f32[1024,4,128]{0,2,1:T(8,128)S(1)} fusion(bf16[1024,8192,1]{1,0,2:T(8,128)(2,1)} %bitcast.3, bf16[4,128,8192]{2,1,0:T(8,128)(2,1)} %bitcast.86), kind=kOutput, calls=%fused_computation.113 | convolution fusion | flops 8589934592 | bytes 27262976 | tf_op jit(solution)/shard_map/dot_general | solution.py:90
  365.0 2.7 convert_element_type.78
  367.6 2.5 copy.15
  370.1 3.6 all-to-all-done.1
  373.7 5.0 fusion.1
  378.7 5.0 fusion.6
  383.8 6.2 %fusion.35 = f32[1,1,4,256,128]{4,3,2,1,0:T(8,128)S(1)} fusion(f32[4,256,4096]{2,1,0:T(8,128)S(1)} %get-tuple-element.26, f32[4,256]{1,0:T(4,128)S(1)} %broadcast_maximum_fusion.2, pred[256,4096]{1,0:T(8,128)(4,1)S(1)} %copy-done.2, bf16[4096,256]{1,0:T(8,128)(2,1)} %bitcast.10), kind=kOutput, calls=%fused_computation.45 | convolution fusion | flops 1094713344 | bytes 19402752 | tf_op jit(solution)/shard_map/ghqk,kgd->ghqd/dot_general | solution.py:137
  390.0 4.9 fusion.2
  395.0 5.1 fusion.8
  400.0 6.1 %fusion.38 = f32[1,1,4,256,128]{4,3,2,1,0:T(8,128)S(1)} fusion(f32[4,256,4096]{2,1,0:T(8,128)S(1)} %get-tuple-element.24, f32[4,256]{1,0:T(4,128)S(1)} %broadcast_maximum_fusion.1, pred[256,4096]{1,0:T(8,128)(4,1)S(1)} %get-tuple-element.17, bf16[4096,256]{1,0:T(8,128)(2,1)} %bitcast.10), kind=kOutput, calls=%fused_computation.46 | convolution fusion | flops 1094713344 | bytes 19402752 | tf_op jit(solution)/shard_map/ghqk,kgd->ghqd/dot_general | solution.py:137
  406.1 4.7 fusion.3
  410.9 5.4 fusion.10
  416.3 6.1 %fusion.41 = f32[1,1,4,256,128]{4,3,2,1,0:T(8,128)S(1)} fusion(f32[4,256,4096]{2,1,0:T(8,128)S(1)} %get-tuple-element.22, f32[4,256]{1,0:T(4,128)S(1)} %broadcast_maximum_fusion, pred[256,4096]{1,0:T(8,128)(4,1)S(1)} %get-tuple-element.18, bf16[4096,256]{1,0:T(8,128)(2,1)} %bitcast.10), kind=kOutput, calls=%fused_computation.47 | convolution fusion | flops 1094713344 | bytes 19402752 | tf_op jit(solution)/shard_map/ghqk,kgd->ghqd/dot_general | solution.py:137
  422.5 4.7 fusion
  427.2 6.1 %fusion.32 = f32[1,1,4,256,128]{4,3,2,1,0:T(8,128)S(1)} fusion(f32[4,256,4096]{2,1,0:T(8,128)S(1)} %get-tuple-element.28, f32[4,256]{1,0:T(4,128)S(1)} %broadcast_maximum_fusion.3, pred[256,4096]{1,0:T(8,128)(4,1)S(1)} %get-tuple-element.15, bf16[4096,256]{1,0:T(8,128)(2,1)} %bitcast.10), kind=kOutput, calls=%fused_computation.44 | convolution fusion | flops 1094713344 | bytes 19402752 | tf_op jit(solution)/shard_map/ghqk,kgd->ghqd/dot_general | solution.py:137
  433.3 5.2 fusion.4
  440.2 15.3 %convolution_convert_fusion = bf16[1024,8192]{1,0:T(8,128)(2,1)} fusion(bf16[512,8192]{1,0:T(8,128)(2,1)} %param.10, bf16[128,8,4,128]{3,2,1,0:T(4,128)(2,1)S(1)} %bitcast.92), kind=kOutput, calls=%fused_computation.8 | convolution fusion | flops 8598323200 | bytes 26214400 | tf_op jit(solution)/shard_map/dot_general | solution.py:152
  455.4 110.5 %reduce-scatter.2.cloned.1.call-done = bf16[64,8192]{1,0:T(8,128)(2,1)} async-done(((bf16[1024,8192]{1,0:T(8,128)(2,1)}), bf16[64,8192]{1,0:T(8,128)(2,1)}) %reduce-scatter.2.cloned.1.call-update) | async-done | bytes 1048592 | tf_op jit(solution)/shard_map/reduce_scatter | solution.py:151
  (39 shorter events, 6.5 us)
Async XLA Ops:
  6.5 266.1 %copy-start = (bf16[8192,128]{1,0:T(8,128)(2,1)S(1)}, bf16[8192,128]{1,0:T(8,128)(2,1)}, u32[]{:S(2)}) copy-start(bf16[8192,128]{1,0:T(8,128)(2,1)} %param.9) | copy-start | bytes 6291460
  15.7 7.8 %copy-start.5 = (s32[8]{0:T(128)S(1)}, s32[8]{0:T(128)}, u32[]{:S(2)}) copy-start(s32[8]{0:T(128)} %param.11) | copy-start | bytes 100
  15.7 256.9 %all-to-all-start = ((bf16[16,64,8192]{2,1,0:T(8,128)(2,1)}), bf16[16,64,8192]{2,1,0:T(8,128)(2,1)}, u32[]{:S(2)}, u32[]{:S(2)}) async-start(bf16[16,64,8192]{2,1,0:T(8,128)(2,1)} %stack.22), calls=%async_computation | async-start | bytes 33554432 | tf_op jit(solution)/shard_map/all_to_all | solution.py:85
  23.5 313.6 %all-gather.2.cloned.1.call-start = ((), (), s32[]{:S(2)}) async-start(), calls=%async_computation.3 | async-start | bytes 4456448 | tf_op jit(solution)/shard_map/all_gather | solution.py:97
  343.6 30.1 %all-to-all-start.1 = ((bf16[4,1024,256]{2,1,0:T(8,128)(2,1)}), bf16[4,1024,256]{2,1,0:T(8,128)(2,1)}, u32[]{:S(2)}, u32[]{:S(2)}) async-start(bf16[4,1024,256]{2,1,0:T(8,128)(2,1)} %broadcast_in_dim.65), calls=%async_computation.1 | async-start | bytes 4194304 | tf_op jit(solution)/shard_map/all_to_all | solution.py:14
  348.9 217.1 %reduce-scatter.2.cloned.1.call-start = ((), (), s32[]{:S(2)}) async-start(), calls=%async_computation.4 | async-start | bytes 17825792 | tf_op jit(solution)/shard_map/reduce_scatter | solution.py:151
  349.1 14.4 %copy-start.3 = (f32[1024,64]{0,1:T(8,128)S(1)}, f32[1024,64]{0,1:T(8,128)}, u32[]{:S(2)}) copy-start(f32[1024,64]{0,1:T(8,128)} %get-tuple-element.20) | copy-start | bytes 786436
  373.7 5.0 copy-start.2
  383.8 6.2 %copy-start.4 = (bf16[4,256,1,4,128]{4,1,3,2,0:T(8,128)(2,1)S(1)}, bf16[4,256,1,4,128]{4,1,3,2,0:T(8,128)(2,1)}, u32[]{:S(2)}) copy-start(bf16[4,256,1,4,128]{4,1,3,2,0:T(8,128)(2,1)} %copy.15) | copy-start | bytes 3145732
  440.1 125.8 %copy-start.1 = (bf16[8192,128]{1,0:T(8,128)(2,1)S(1)}, bf16[8192,128]{1,0:T(8,128)(2,1)}, u32[]{:S(2)}) copy-start(bf16[8192,128]{1,0:T(8,128)(2,1)} %param.9) | copy-start | bytes 6291460
Sparse Core Ops, SparseCore 0:
  286.1 50.8 all-gather.1
  455.6 110.3 reduce-scatter.1
